TPU v7x, 128 devices: a whole 4x4x4 slice. The times are simulated.
128 devices in a mesh: dom: 32 (over z, y_lo, x), feat: 4 (over y_hi, core).
Axes of the slice: x: 4, y: 4 (y_hi: 2, y_lo: 2; y = y_hi * 2 + y_lo), z: 4, core: 2. Of those that a mesh axis runs over, the one named last changes fastest.
Arguments:
- items: bfloat16 [8192, 1024], P('dom', 'feat'), may hold values from -6 to 6
- self_ids: int32 [8192], P('dom'), may hold values from 0 to 8191
- neighbor_ids: int32 [8192, 50], P('dom'), may hold values from 0 to 8191
- visit_counts: int32 [8192, 50], P('dom'), may hold values from 1 to 63
- w_self: bfloat16 [1024, 1024], P('feat'), may hold values from -0.1875 to 0.1875
- w_neighbor: bfloat16 [1024, 1024], P('feat'), may hold values from -0.75 to 0.75
- bias: float32 [1024], replicated, may hold values from -3 to 3
Outputs:
- embedding: float32 [8192, 1024], P('dom', 'feat')
All inputs are finite; a program needn't handle non-finite values.
Results may differ from a plain program's by a relative error of at most 0.0018.
Values may be sent and summed in bfloat16 or wider, within the bound.
No kernel may reach another device: no remote copies, remote signals or barrier semaphores. Data moves between devices by JAX's collectives and lax.ppermute only.
A program may use at most 64 MiB of HBM per device.

v0:
```python
import jax
import jax.numpy as jnp
from jax import lax
from jax.sharding import Mesh
from jax.sharding import PartitionSpec as P

DOM = ("dom_0", "dom_1", "dom_2")


def joined_along(tiles, dim):
    lengths = list(tiles.shape[1:])
    lengths[dim] *= tiles.shape[0]
    return jnp.moveaxis(tiles, 0, dim).reshape(lengths)


def stacked_from(value, axes, sequence):
    tiles = value[None]
    for k in sequence:
        tiles = lax.all_gather(tiles, axes[k], axis=0, tiled=True)
    block = [lax.axis_size(axes[k]) for k in reversed(sequence)]
    tiles = tiles.reshape(*block, *value.shape)
    turned = sorted(range(len(sequence)), key=lambda place: sequence[len(sequence) - 1 - place])
    return tiles.transpose(*turned, *range(len(sequence), tiles.ndim)).reshape(-1, *value.shape)


def gathered_by_axis(value, axes, sequence, dim):
    return joined_along(stacked_from(value, axes, sequence), dim)


def in_blocks(value, dim, length):
    before, after = (value.shape[:dim], value.shape[dim + 1 :])
    return jnp.moveaxis(value.reshape(*before, length, -1, *after), dim, 0)


def sent_and_summed(value, axis, dim):
    length = lax.axis_size(axis)
    tiles = lax.all_to_all(in_blocks(value, dim, length), axis, 0, 0, tiled=True)
    return jnp.sum(tiles, axis=0)


def copy_for_each(value, axis):
    length = lax.axis_size(axis)
    return lax.all_to_all(
        jnp.broadcast_to(value[None], (length, *value.shape)), axis, 0, 0, tiled=True
    )


def of_everyone(value, axis):
    everything = copy_for_each(value, axis)
    return jnp.sum(everything, axis=0)


def count_block(target_ids, target_weights, width):
    columns = jnp.arange(width, dtype=jnp.int32)
    match = target_ids[:, :, None] == columns[None, None, :]
    block = jnp.sum(jnp.where(match, target_weights[:, :, None], 0.0), axis=1)
    return block.astype(jnp.bfloat16)


def shards(items, self_ids, neighbor_ids, visit_counts, w_self, w_neighbor, bias):
    batch_rows = self_ids.shape[0]
    counts_float = visit_counts.astype(jnp.float32)
    self_column = self_ids[:, None]
    self_weight = jnp.ones((batch_rows, 1), jnp.float32)
    piece = gathered_by_axis(items, DOM, (1, 0, 2), 0)
    own_block = count_block(self_column, self_weight, piece.shape[0])
    nbr_block = count_block(neighbor_ids, counts_float, piece.shape[0])
    weights = jnp.concatenate([own_block, nbr_block], axis=0)
    sums = jnp.dot(weights, piece, preferred_element_type=jnp.float32)
    own = sums[:batch_rows].astype(jnp.bfloat16)
    nbr_sum = sums[batch_rows:]
    total = jnp.sum(counts_float, axis=1)
    pooled = (nbr_sum / total[:, None]).astype(jnp.bfloat16)
    partial_pre = jnp.dot(own, w_self, preferred_element_type=jnp.float32) + jnp.dot(
        pooled, w_neighbor, preferred_element_type=jnp.float32
    )
    out_share = bias.shape[0] // lax.axis_size("feat")
    column_first = lax.axis_index("feat") * out_share
    pre = sent_and_summed(partial_pre, "feat", 1)
    my_bias = lax.dynamic_slice_in_dim(bias, column_first, out_share, 0)
    hidden = jnp.maximum(pre + my_bias[None, :], 0.0)
    squares = of_everyone(jnp.sum(hidden * hidden, axis=1, keepdims=True), "feat")
    scale = jnp.sqrt(squares / bias.shape[0] + 1e-06)
    return hidden / scale


def solution(mesh):
    torus = Mesh(
        mesh.devices.reshape(4, 2, 4, mesh.shape["feat"]), ("dom_0", "dom_1", "dom_2", "feat")
    )
    placed = (
        P(DOM, "feat"),
        P(DOM),
        P(DOM, None),
        P(DOM, None),
        P("feat", None),
        P("feat", None),
        P(),
    )
    return jax.shard_map(
        shards, mesh=torus, in_specs=placed, out_specs=P(DOM, "feat"), check_vma=False
    )
```

profile of v0, /device:TPU:1, one launch (start us, length us, event | category | flops | bytes accessed | tf_op | source)
XLA Modules:
  0.0 195.1 jit_solution(11336127264499368638)
XLA Ops:
  6.5 0.0 all-gather.4.cloned.1.call-start
  6.5 7.9 %all-gather = bf16[512,256]{1,0:T(8,128)(2,1)} all-gather(bf16[256,256]{1,0:T(8,128)(2,1)} %param.7), channel_id=2, replica_groups=mesh['dom_0'=4,'dom_1'=2,'dom_2'=4,'feat'=4] {'dom_1'}, dimensions={0}, use_global_device_ids=true | all-gather | bytes 393216 | tf_op jit(solution)/shard_map/all_gather | solution.py:19
  14.5 0.0 all-gather.4.cloned.1.call-update
  14.5 0.0 all-gather.6.cloned.1.call-start
  14.6 0.8 convert_element_type.14
  15.4 0.8 convert_reduce_fusion
  16.2 3.7 %select_convert_fusion = bf16[256,8192]{1,0:T(8,128)(2,1)} fusion(s32[256]{0:T(256)} %param.8), kind=kLoop, calls=%fused_computation.6 | loop fusion | flops 6291456 | bytes 4195328 | tf_op jit(solution)/shard_map/convert_element_type | solution.py:57
  20.0 19.6 %all-gather.4.cloned.1.call-done = bf16[8,256,256]{2,1,0:T(8,128)(2,1)} async-done(((bf16[2,256,256]{2,1,0:T(8,128)(2,1)}), bf16[8,256,256]{2,1,0:T(8,128)(2,1)}) %all-gather.4.cloned.1.call-update) | async-done | bytes 1048592 | tf_op jit(solution)/shard_map/all_gather | solution.py:19
  39.6 0.0 all-gather.6.cloned.1.call-update
  39.6 108.8 %select_reduce_fusion = bf16[256,8192]{1,0:T(8,128)(2,1)} fusion(f32[256,50]{0,1:T(8,128)S(1)} %convert_element_type.14, s32[256,50]{0,1:T(8,128)S(1)} %copy-done.4), kind=kLoop, calls=%fused_computation | loop fusion | flops 312475648 | bytes 4296704 | tf_op jit(solution)/shard_map/reduce_sum | solution.py:56
  148.5 2.8 %copy.19 = bf16[4,2,4,256,256]{4,3,2,1,0:T(8,128)(2,1)S(1)} copy(bf16[4,2,4,256,256]{4,3,1,0,2:T(8,128)(2,1)} %bitcast.15) | data formatting | bytes 8388608 | tf_op jit(solution)/shard_map/transpose | solution.py:23
  151.2 0.7 copy-done.1
  151.9 1.3 copy-done.2
  153.2 2.3 %fusion = f32[512,256]{1,0:T(8,128)S(1)} fusion(bf16[8192,256]{1,0:T(8,128)(2,1)S(1)} %bitcast.16, bf16[256,8192]{1,0:T(8,128)(2,1)S(1)} %copy-done.2, bf16[256,8192]{1,0:T(8,128)(2,1)S(1)} %copy-done.1), kind=kOutput, calls=%fused_computation.2 | convolution fusion | flops 2164260864 | bytes 13107200 | tf_op jit(solution)/shard_map/dot_general | solution.py:69
  155.5 0.3 fusion.6
  155.9 0.3 convolution_add_fusion
  156.2 1.1 copy.23
  157.3 7.0 %all-to-all-start = ((f32[4,256,256]{2,1,0:T(8,128)}), f32[4,256,256]{2,1,0:T(8,128)S(1)}, u32[]{:S(2)}, u32[]{:S(2)}) async-start(f32[4,256,256]{2,1,0:T(8,128)} %bitcast.14), calls=%async_computation | async-start | bytes 2097152 | tf_op jit(solution)/shard_map/all_to_all | solution.py:37
  164.3 0.8 dynamic_slice.3
  165.1 14.2 %all-to-all-done = f32[4,256,256]{2,1,0:T(8,128)S(1)} async-done(((f32[4,256,256]{2,1,0:T(8,128)}), f32[4,256,256]{2,1,0:T(8,128)S(1)}, u32[]{:S(2)}, u32[]{:S(2)}) %all-to-all-start) | async-done | bytes 1048608 | tf_op jit(solution)/shard_map/all_to_all | solution.py:37
  179.3 0.1 reduce_sum.51
  179.4 0.1 multiply_reduce_fusion
  179.5 7.9 %all_to_all.10 = f32[4,256,1]{1,2,0:T(1,128)S(1)} all-to-all(f32[4,256,1]{1,2,0:T(1,128)S(1)} %broadcast_in_dim.43), channel_id=1, replica_groups=mesh['dom_0'=4,'dom_1'=2,'dom_2'=4,'feat'=4] {'feat'}, dimensions={0} | all-to-all | bytes 8192 | tf_op jit(solution)/shard_map/all_to_all | solution.py:43
  187.4 0.8 fusion.5
  (12 shorter events, 0.1 us)
Async XLA Ops:
  6.5 149.0 %copy-start = (bf16[256,1024]{1,0:T(8,128)(2,1)S(1)}, bf16[256,1024]{1,0:T(8,128)(2,1)}, u32[]{:S(2)}) copy-start(bf16[256,1024]{1,0:T(8,128)(2,1)} %param.11) | copy-start | bytes 1572868
  6.5 33.1 %copy-start.4 = (s32[256,50]{0,1:T(8,128)S(1)}, s32[256,50]{0,1:T(8,128)}, u32[]{:S(2)}) copy-start(s32[256,50]{0,1:T(8,128)} %param.9) | copy-start | bytes 153604
  6.5 33.0 %all-gather.4.cloned.1.call-start = ((), (), s32[]{:S(2)}) async-start(), calls=%async_computation.2 | async-start | bytes 1310720 | tf_op jit(solution)/shard_map/all_gather | solution.py:19
  14.5 133.9 %all-gather.6.cloned.1.call-start = ((), (), s32[]{:S(2)}) async-start(), calls=%async_computation.3 | async-start | bytes 5242880 | tf_op jit(solution)/shard_map/all_gather | solution.py:19
  148.4 3.4 %copy-start.1 = (bf16[256,8192]{1,0:T(8,128)(2,1)S(1)}, bf16[256,8192]{1,0:T(8,128)(2,1)}, u32[]{:S(2)}) copy-start(bf16[256,8192]{1,0:T(8,128)(2,1)} %select_convert_fusion) | copy-start | bytes 12582916
  148.4 4.7 %copy-start.2 = (bf16[256,8192]{1,0:T(8,128)(2,1)S(1)}, bf16[256,8192]{1,0:T(8,128)(2,1)}, u32[]{:S(2)}) copy-start(bf16[256,8192]{1,0:T(8,128)(2,1)} %select_reduce_fusion) | copy-start | bytes 12582916
  153.2 2.7 %copy-start.3 = (bf16[256,1024]{1,0:T(8,128)(2,1)S(1)}, bf16[256,1024]{1,0:T(8,128)(2,1)}, u32[]{:S(2)}) copy-start(bf16[256,1024]{1,0:T(8,128)(2,1)} %param.12) | copy-start | bytes 1572868
  157.3 22.0 %all-to-all-start = ((f32[4,256,256]{2,1,0:T(8,128)}), f32[4,256,256]{2,1,0:T(8,128)S(1)}, u32[]{:S(2)}, u32[]{:S(2)}) async-start(f32[4,256,256]{2,1,0:T(8,128)} %bitcast.14), calls=%async_computation | async-start | bytes 2097152 | tf_op jit(solution)/shard_map/all_to_all | solution.py:37
Sparse Core Ops, SparseCore 0:
  14.6 24.8 all-gather.3
  41.2 50.2 all-gather.5
where the time goes:
time: 195 us
  other arithmetic  115 us (59%)
  waiting for transfers between devices  33.9 us (17%)
  blocking collectives  15.8 us (8%)
  between operations  13.5 us (7%)
  starting transfers between devices  7.07 us (4%)
  local copies, waits for them, and re-layouts  6.58 us (3%)
  matrix products  2.99 us (2%)
    reduce_sum x1, other arithmetic, count_block(): block = jnp.sum(jnp.where(match, target_weights[:, :, None], 0.0), axis=1)  109 us
    all_gather x2, waiting for transfers between devices, stacked_from(): tiles = lax.all_gather(tiles, axes[k], axis=0, tiled=True)  19.6 us
    all_to_all x1, waiting for transfers between devices, sent_and_summed(): lax.all_to_all(in_blocks(value, dim, length), axis, 0, 0, tiled=True)  14.2 us
    all_gather x1, blocking collectives, stacked_from(): tiles = lax.all_gather(tiles, axes[k], axis=0, tiled=True)  7.94 us
    all_to_all x1, blocking collectives, copy_for_each(): lax.all_to_all(jnp.broadcast_to(value[None], (length, *value.shape)), axi...  7.91 us
    all_to_all x1, starting transfers between devices, sent_and_summed(): lax.all_to_all(in_blocks(value, dim, length), axis, 0, 0, tiled=True)  7.03 us
  transfers between devices with their start and end apart: 3, of which 2 were waited for; matrix products, arithmetic and copies ran while one was open for 59% of the time, Pallas kernels for 0%

commit v1 on v0

--- a/solution.py
+++ b/solution.py
@@ -16,7 +16,9 @@
 def stacked_from(value, axes, sequence):
     tiles = value[None]
     for k in sequence:
-        tiles = lax.all_gather(tiles, axes[k], axis=0, tiled=True)
+        tiles = jnp.concatenate(
+            lax.all_to_all(jnp.stack([tiles] * lax.axis_size(axes[k])), axes[k], 0, 0), axis=0
+        )
     block = [lax.axis_size(axes[k]) for k in reversed(sequence)]
     tiles = tiles.reshape(*block, *value.shape)
     turned = sorted(range(len(sequence)), key=lambda place: sequence[len(sequence) - 1 - place])

time: 195 us -> 188 us (0.964)
  between operations: 13.5 us -> 0.11 us
  starting transfers between devices: 7.07 us -> 18 us
  waiting for transfers between devices: 33.9 us -> 27.3 us
  local copies, waits for them, and re-layouts: 6.58 us -> 10.1 us
    all_gather x2 -> x0, waiting for transfers between devices: 19.6 us -> none  [stacked_from(): tiles = lax.all_gather(tiles, axes[k], axis=0, tiled=True)]
    all_to_all x0 -> x2, waiting for transfers between devices: none -> 13.1 us  [stacked_from(): lax.all_to_all(jnp.stack([tiles] * lax.axis_size(axes[k])), axes[k], 0, 0)]
    all_to_all x0 -> x2, starting transfers between devices: none -> 10.3 us  [stacked_from(): lax.all_to_all(jnp.stack([tiles] * lax.axis_size(axes[k])), axes[k], 0, 0)]
    all_gather x1 -> x0, blocking collectives: 7.94 us -> none  [stacked_from(): tiles = lax.all_gather(tiles, axes[k], axis=0, tiled=True)]
    all_to_all x0 -> x1, blocking collectives: none -> 7.21 us  [stacked_from(): lax.all_to_all(jnp.stack([tiles] * lax.axis_size(axes[k])), axes[k], 0, 0)]
    another operation x0 -> x2, local copies, waits for them, and re-layouts: none -> 3.51 us  [stacked_from(): jnp.stack([tiles] * lax.axis_size(axes[k]))]
    all_to_all x0 -> x1, local copies, waits for them, and re-layouts: none -> 2.76 us  [stacked_from(): lax.all_to_all(jnp.stack([tiles] * lax.axis_size(axes[k])), axes[k], 0, 0)]
    transpose x1 -> x0, local copies, waits for them, and re-layouts: 2.76 us -> none  [stacked_from(): tiles.transpose(*turned, *range(len(sequence), tiles.ndim))]
  transfers between devices with their start and end apart: 3 -> 3, of which waited for: 2 -> 2; matrix products, arithmetic and copies ran while one was open for 59% -> 60% of each run, Pallas kernels for 0% -> 0%
where the time goes in v1:
time: 188 us
  other arithmetic  114 us (61%)
  waiting for transfers between devices  27.3 us (15%)
  starting transfers between devices  18 us (10%)
  blocking collectives  15.1 us (8%)
  local copies, waits for them, and re-layouts  10.1 us (5%)
  matrix products  2.98 us (2%)
    reduce_sum x1, other arithmetic, count_block(): block = jnp.sum(jnp.where(match, target_weights[:, :, None], 0.0), axis=1)  109 us
    all_to_all x1, waiting for transfers between devices, sent_and_summed(): lax.all_to_all(in_blocks(value, dim, length), axis, 0, 0, tiled=True)  14.2 us
    all_to_all x2, waiting for transfers between devices, stacked_from(): lax.all_to_all(jnp.stack([tiles] * lax.axis_size(axes[k])), axes[k], 0, 0)  13.1 us
    all_to_all x2, starting transfers between devices, stacked_from(): lax.all_to_all(jnp.stack([tiles] * lax.axis_size(axes[k])), axes[k], 0, 0)  10.3 us
    all_to_all x1, blocking collectives, copy_for_each(): lax.all_to_all(jnp.broadcast_to(value[None], (length, *value.shape)), axi...  7.91 us
    all_to_all x1, starting transfers between devices, sent_and_summed(): lax.all_to_all(in_blocks(value, dim, length), axis, 0, 0, tiled=True)  7.65 us
    all_to_all x1, blocking collectives, stacked_from(): lax.all_to_all(jnp.stack([tiles] * lax.axis_size(axes[k])), axes[k], 0, 0)  7.21 us
  transfers between devices with their start and end apart: 3, of which 2 were waited for; matrix products, arithmetic and copies ran while one was open for 60% of the time, Pallas kernels for 0%

profile of v1, /device:TPU:1, one launch (start us, length us, event | category | flops | bytes accessed | tf_op | source)
XLA Modules:
  0.0 187.6 jit_solution(8486941571046100140)
XLA Ops:
  0.0 1.1 pad_maximum_fusion
  1.1 7.2 %all_to_all.25 = bf16[2,1,256,256]{3,2,1,0:T(8,128)(2,1)S(1)} all-to-all(bf16[2,1,256,256]{3,2,1,0:T(8,128)(2,1)S(1)} %pad_maximum_fusion), channel_id=1, replica_groups=mesh['dom_0'=4,'dom_1'=2,'dom_2'=4,'feat'=4] {'dom_1'}, dimensions={0} | all-to-all | bytes 524288 | tf_op jit(solution)/shard_map/all_to_all | solution.py:20
  8.3 1.1 stack.10
  9.3 5.4 %all-to-all-start.1 = ((bf16[4,2,256,256]{3,2,1,0:T(8,128)(2,1)}), bf16[4,2,256,256]{3,2,1,0:T(8,128)(2,1)S(1)}, u32[]{:S(2)}, u32[]{:S(2)}) async-start(bf16[4,2,256,256]{3,2,1,0:T(8,128)(2,1)} %stack.10), calls=%async_computation.1 | async-start | bytes 2097152 | tf_op jit(solution)/shard_map/all_to_all | solution.py:20
  14.7 13.1 %all-to-all-done.1 = bf16[4,2,256,256]{3,2,1,0:T(8,128)(2,1)S(1)} async-done(((bf16[4,2,256,256]{3,2,1,0:T(8,128)(2,1)}), bf16[4,2,256,256]{3,2,1,0:T(8,128)(2,1)S(1)}, u32[]{:S(2)}, u32[]{:S(2)}) %all-to-all-start.1) | async-done | bytes 1048608 | tf_op jit(solution)/shard_map/all_to_all | solution.py:20
  27.8 2.5 %stack.11 = bf16[4,8,256,256]{3,2,1,0:T(8,128)(2,1)} broadcast(bf16[8,256,256]{2,1,0:T(8,128)(2,1)S(1)} %bitcast.18), dimensions={1,2,3} | broadcast | bytes 5242880 | tf_op jit(solution)/shard_map/stack | solution.py:20
  30.3 5.0 %all-to-all-start.2 = ((bf16[4,8,256,256]{3,2,1,0:T(8,128)(2,1)}), bf16[4,8,256,256]{3,2,1,0:T(8,128)(2,1)}, u32[]{:S(2)}, u32[]{:S(2)}) async-start(bf16[4,8,256,256]{3,2,1,0:T(8,128)(2,1)} %stack.11), calls=%async_computation.2 | async-start | bytes 8388608 | tf_op jit(solution)/shard_map/all_to_all | solution.py:20
  35.3 0.0 copy-start.6
  35.3 108.8 %select_reduce_fusion = bf16[256,8192]{1,0:T(8,128)(2,1)} fusion(f32[256,50]{0,1:T(8,128)S(1)} %convert_element_type.14, s32[256,50]{0,1:T(8,128)S(1)} %copy-done.5), kind=kLoop, calls=%fused_computation | loop fusion | flops 312475648 | bytes 4296704 | tf_op jit(solution)/shard_map/reduce_sum | solution.py:58
  144.1 3.1 %select_convert_fusion = bf16[256,8192]{1,0:T(8,128)(2,1)} fusion(s32[256]{0:T(256)S(1)} %copy-done.6), kind=kLoop, calls=%fused_computation.6 | loop fusion | flops 6291456 | bytes 4195328 | tf_op jit(solution)/shard_map/convert_element_type | solution.py:59
  147.2 2.8 %copy.16 = bf16[4,8,256,256]{3,2,0,1:T(8,128)(2,1)S(1)} copy(bf16[4,8,256,256]{3,2,1,0:T(8,128)(2,1)} %all-to-all-done.2) | data formatting | bytes 8388608 | tf_op jit(solution)/shard_map/all_to_all | solution.py:20
  150.0 0.7 copy-done.1
  150.6 1.3 copy-done.2
  151.9 2.3 %fusion = f32[512,256]{1,0:T(8,128)S(1)} fusion(bf16[8192,256]{1,0:T(8,128)(2,1)S(1)} %bitcast.19, bf16[256,8192]{1,0:T(8,128)(2,1)S(1)} %copy-done.2, bf16[256,8192]{1,0:T(8,128)(2,1)S(1)} %copy-done.1), kind=kOutput, calls=%fused_computation.2 | convolution fusion | flops 2164260864 | bytes 13107200 | tf_op jit(solution)/shard_map/dot_general | solution.py:71
  154.3 0.3 fusion.6
  154.6 0.3 convolution_add_fusion
  154.9 1.1 copy.20
  156.0 7.7 %all-to-all-start.3 = ((f32[4,256,256]{2,1,0:T(8,128)}), f32[4,256,256]{2,1,0:T(8,128)S(1)}, u32[]{:S(2)}, u32[]{:S(2)}) async-start(f32[4,256,256]{2,1,0:T(8,128)} %bitcast.17), calls=%async_computation.3 | async-start | bytes 2097152 | tf_op jit(solution)/shard_map/all_to_all | solution.py:39
  163.7 0.8 dynamic_slice.3
  164.4 14.2 %all-to-all-done.3 = f32[4,256,256]{2,1,0:T(8,128)S(1)} async-done(((f32[4,256,256]{2,1,0:T(8,128)}), f32[4,256,256]{2,1,0:T(8,128)S(1)}, u32[]{:S(2)}, u32[]{:S(2)}) %all-to-all-start.3) | async-done | bytes 1048608 | tf_op jit(solution)/shard_map/all_to_all | solution.py:39
  178.7 0.1 reduce_sum.51
  178.7 0.1 multiply_reduce_fusion
  178.9 7.9 %all_to_all.26 = f32[4,256,1]{1,2,0:T(1,128)S(1)} all-to-all(f32[4,256,1]{1,2,0:T(1,128)S(1)} %broadcast_in_dim.39), channel_id=1, replica_groups=mesh['dom_0'=4,'dom_1'=2,'dom_2'=4,'feat'=4] {'feat'}, dimensions={0} | all-to-all | bytes 8192 | tf_op jit(solution)/shard_map/all_to_all | solution.py:45
  186.8 0.8 fusion.5
  (17 shorter events, 0.1 us)
Async XLA Ops:
  0.0 154.3 %copy-start = (bf16[256,1024]{1,0:T(8,128)(2,1)S(1)}, bf16[256,1024]{1,0:T(8,128)(2,1)}, u32[]{:S(2)}) copy-start(bf16[256,1024]{1,0:T(8,128)(2,1)} %param.11) | copy-start | bytes 1572868
  0.0 14.7 %copy-start.4 = (s32[256,50]{0,1:T(8,128)S(1)}, s32[256,50]{0,1:T(8,128)}, u32[]{:S(2)}) copy-start(s32[256,50]{0,1:T(8,128)} %param.10) | copy-start | bytes 153604
  9.3 18.5 %all-to-all-start.1 = ((bf16[4,2,256,256]{3,2,1,0:T(8,128)(2,1)}), bf16[4,2,256,256]{3,2,1,0:T(8,128)(2,1)S(1)}, u32[]{:S(2)}, u32[]{:S(2)}) async-start(bf16[4,2,256,256]{3,2,1,0:T(8,128)(2,1)} %stack.10), calls=%async_computation.1 | async-start | bytes 2097152 | tf_op jit(solution)/shard_map/all_to_all | solution.py:20
  30.3 5.0 %copy-start.5 = (s32[256,50]{0,1:T(8,128)S(1)}, s32[256,50]{0,1:T(8,128)}, u32[]{:S(2)}) copy-start(s32[256,50]{0,1:T(8,128)} %param.9) | copy-start | bytes 153604
  30.3 116.9 %all-to-all-start.2 = ((bf16[4,8,256,256]{3,2,1,0:T(8,128)(2,1)}), bf16[4,8,256,256]{3,2,1,0:T(8,128)(2,1)}, u32[]{:S(2)}, u32[]{:S(2)}) async-start(bf16[4,8,256,256]{3,2,1,0:T(8,128)(2,1)} %stack.11), calls=%async_computation.2 | async-start | bytes 8388608 | tf_op jit(solution)/shard_map/all_to_all | solution.py:20
  35.3 108.8 %copy-start.6 = (s32[256]{0:T(256)S(1)}, s32[256]{0:T(256)}, u32[]{:S(2)}) copy-start(s32[256]{0:T(256)} %param.8) | copy-start | bytes 3076
  147.2 3.5 %copy-start.1 = (bf16[256,8192]{1,0:T(8,128)(2,1)S(1)}, bf16[256,8192]{1,0:T(8,128)(2,1)}, u32[]{:S(2)}) copy-start(bf16[256,8192]{1,0:T(8,128)(2,1)} %select_convert_fusion) | copy-start | bytes 12582916
  147.2 4.7 %copy-start.2 = (bf16[256,8192]{1,0:T(8,128)(2,1)S(1)}, bf16[256,8192]{1,0:T(8,128)(2,1)}, u32[]{:S(2)}) copy-start(bf16[256,8192]{1,0:T(8,128)(2,1)} %select_reduce_fusion) | copy-start | bytes 12582916
  151.9 2.7 %copy-start.3 = (bf16[256,1024]{1,0:T(8,128)(2,1)S(1)}, bf16[256,1024]{1,0:T(8,128)(2,1)}, u32[]{:S(2)}) copy-start(bf16[256,1024]{1,0:T(8,128)(2,1)} %param.12) | copy-start | bytes 1572868
  156.0 22.6 %all-to-all-start.3 = ((f32[4,256,256]{2,1,0:T(8,128)}), f32[4,256,256]{2,1,0:T(8,128)S(1)}, u32[]{:S(2)}, u32[]{:S(2)}) async-start(f32[4,256,256]{2,1,0:T(8,128)} %bitcast.17), calls=%async_computation.3 | async-start | bytes 2097152 | tf_op jit(solution)/shard_map/all_to_all | solution.py:39
